TPU v7x, 32 devices: a whole 2x2x4 slice. The times are simulated.
32 devices in a mesh: box: 8 (over z, x), path: 4 (over y, core).
Axes of the slice: x: 2, y: 2, z: 4, core: 2. Of those that a mesh axis runs over, the one named last changes fastest.
Arguments:
- features: float32 [1024, 9, 128], P('box'), may hold values from -6 to 6
- positions: float32 [3, 1024], P(None, 'box'), may hold values from 0 to 96, as said below
- cotangent: bfloat16 [1024, 9, 128], P('box'), may hold values from -6 to 6
- weights: float32 [8, 8, 128], P('path'), may hold values from -2 to 2
- neighbours: int32 [16, 3], P('box'), may hold values from 0 to 3, as said below
- send_list: int32 [8, 2], P('box'), may hold values from 0 to 1, as said below
Outputs:
- grad_features: float32 [1024, 9, 128], P(('box', 'path'))
- grad_weights: float32 [8, 8, 128], P('path')
Inputs may be any that keep to these rules, and one draw needn't show every extreme that they name: `positions`: stored block s of box b has a place g = b * 2 + (a permutation of 0 to 1 within the box) along a chain; its atoms lie near the points of a grid of spacing 1.5 with 4 x 4 points across and 4 along the third coordinate, the first coordinate between 6 g and 6 g + 6, each moved by at most 0.35 in each coordinate. Blocks whose places differ by two or more have no atoms within 5 of each other. `neighbours`: row g lists the block itself (its stored index), the block one place before it and the block one place after it along the chain, as table indices: below 2 the box's own stored blocks, 2 the block received from the previous box (its last block along the chain), 3 the block received from the next box (its first block along the chain). The relation is symmetric. send_list[b, 0] is the stored index of the first block of box b's stretch of the chain and send_list[b, 1] that of the last.
All inputs are finite; a program needn't handle non-finite values.
Results may differ from a plain program's by a relative error of at most 0.0045.
Values may be sent and summed in bfloat16 or wider, within the bound.
A program may use at most 64 MiB of HBM per device.

v0:
```python
import math
import jax
import jax.numpy as jnp
from jax import lax
from jax.sharding import PartitionSpec as P

BASIS = 8
BLOCK = 64
NEIGHBOURS = 3
PATHS = 8
cutoff_radius = 5.0
edge_scale = 0.2
basis_width = 0.8
root_three = math.sqrt(3.0)
path_terms = [
    [(0, [(0, 0, 1.0)])],
    [(0, [(1, 1, 1.0), (2, 2, 1.0), (3, 3, 1.0)])],
    [(1, [(1, 0, 1.0)]), (2, [(2, 0, 1.0)]), (3, [(3, 0, 1.0)])],
    [(1, [(0, 1, 1.0)]), (2, [(0, 2, 1.0)]), (3, [(0, 3, 1.0)])],
    [
        (4, [(4, 0, 1.0)]),
        (5, [(5, 0, 1.0)]),
        (6, [(6, 0, 1.0)]),
        (7, [(7, 0, 1.0)]),
        (8, [(8, 0, 1.0)]),
    ],
    [
        (4, [(0, 4, 1.0)]),
        (5, [(0, 5, 1.0)]),
        (6, [(0, 6, 1.0)]),
        (7, [(0, 7, 1.0)]),
        (8, [(0, 8, 1.0)]),
    ],
    [
        (1, [(3, 2, 1.0), (2, 3, -1.0)]),
        (2, [(1, 3, 1.0), (3, 1, -1.0)]),
        (3, [(2, 1, 1.0), (1, 2, -1.0)]),
    ],
    [(0, [(4, 4, 1.0), (5, 5, 1.0), (6, 6, 1.0), (7, 7, 1.0), (8, 8, 1.0)])],
]


def with_halo(cells, sides, width):
    for axis, dim in sides:
        count = lax.axis_size(axis)
        ends = count - 1
        head = lax.slice_in_dim(cells, 0, width, axis=dim)
        tail = lax.slice_in_dim(cells, cells.shape[dim] - width, cells.shape[dim], axis=dim)
        cells = jnp.concatenate(
            [
                lax.ppermute(tail, axis, [(i, (i + 1) % count) for i in range(ends)]),
                cells,
                lax.ppermute(head, axis, [((i + 1) % count, i) for i in range(ends)]),
            ],
            axis=dim,
        )
    return cells


def edge_tensor(anchor, target):
    offset = target[:, None, :] - anchor[:, :, None]
    square = jnp.sum(offset * offset, axis=0)
    inside = square > 0.01
    distance = jnp.sqrt(jnp.where(inside, square, 1.0))
    direction = offset / distance[None]
    envelope = jnp.where(
        inside & (distance < cutoff_radius),
        0.5 * (jnp.cos(math.pi * distance / cutoff_radius) + 1.0),
        0.0,
    )
    centres = (jnp.arange(BASIS, dtype=jnp.float32) + 0.5) * (cutoff_radius / BASIS)
    radial = (
        jnp.exp(-jnp.square((distance[None] - centres[:, None, None]) / basis_width))
        * (edge_scale * envelope)[None]
    )
    eastward = direction[0]
    northward = direction[1]
    upward = direction[2]
    harmonics = jnp.stack(
        [
            jnp.ones_like(eastward),
            eastward,
            northward,
            upward,
            root_three * eastward * northward,
            root_three * northward * upward,
            0.5 * (3.0 * upward * upward - 1.0),
            root_three * eastward * upward,
            0.5 * root_three * (eastward * eastward - northward * northward),
        ]
    )
    return (harmonics[:, None] * radial[None]).astype(jnp.bfloat16)


def forward_terms(paths, weights, edge_table, rounded):
    source_rows = rounded.shape[0]
    target_rows = edge_table.shape[2]
    channels = rounded.shape[2]
    outputs = [jnp.zeros((target_rows, channels), jnp.float32) for output in range(9)]
    for weight_slot, path_number in enumerate(paths):
        for output, term_list in path_terms[path_number]:
            pieces = []
            stacked = []
            for harmonic, source, factor in term_list:
                signed = edge_table[harmonic] if factor > 0 else -edge_table[harmonic]
                pieces.append(signed.reshape(BASIS * target_rows, source_rows))
                stacked.append(rounded[:, source, :])
            product = jnp.dot(
                jnp.concatenate(pieces, axis=1),
                jnp.concatenate(stacked, axis=0),
                preferred_element_type=jnp.float32,
            )
            product = product.reshape(BASIS, target_rows, channels)
            outputs[output] = outputs[output] + jnp.sum(
                weights[weight_slot][:, None, :] * product, axis=0
            )
    return jnp.stack(outputs, axis=1)


def transpose_terms(paths, weights, edge_table, cotangent_rows, source_features):
    rows = source_features.shape[0]
    channels = source_features.shape[2]
    outputs = [jnp.zeros((rows, channels), jnp.float32) for output in range(9)]
    weight_parts = []
    for weight_slot, path_number in enumerate(paths):
        weight_part = jnp.zeros((BASIS, channels), jnp.float32)
        for output, term_list in path_terms[path_number]:
            for harmonic, source, factor in term_list:
                gathered = lax.dot_general(
                    edge_table[harmonic],
                    cotangent_rows[:, output, :],
                    (((1,), (0,)), ((), ())),
                    preferred_element_type=jnp.float32,
                )
                outputs[source] = outputs[source] + factor * jnp.sum(
                    weights[weight_slot][:, None, :] * gathered, axis=0
                )
                weight_part = weight_part + factor * jnp.sum(
                    source_features[:, source, :][None] * gathered, axis=1
                )
        weight_parts.append(weight_part)
    return (jnp.stack(outputs, axis=1), jnp.stack(weight_parts, axis=0))


def gate_back(message, cotangent):
    incoming = cotangent.astype(jnp.float32)
    scalar = message[:, 0]
    sigma = jax.nn.sigmoid(scalar)
    slope = sigma * (1.0 + scalar * (1.0 - sigma))
    coupling = jnp.sum(incoming[:, 1:] * message[:, 1:], axis=1)
    leading = incoming[:, 0] * slope + sigma * (1.0 - sigma) * coupling
    others = incoming[:, 1:] * sigma[:, None]
    return jnp.concatenate([leading[:, None], others], axis=1).astype(jnp.bfloat16)


def on_device(features, positions, cotangent, weights, neighbours, send_list):
    local_blocks = neighbours.shape[0]
    local_rows = features.shape[0]
    channels = features.shape[2]
    block_features = features.reshape(local_blocks, BLOCK, 9, channels)
    block_places = positions.reshape(3, local_blocks, BLOCK).transpose(1, 0, 2)
    outgoing = send_list[0]
    padded_features, padded_places = (
        with_halo(block_features[outgoing], (("box", 0),), 1),
        with_halo(block_places[outgoing], (("box", 0),), 1),
    )
    table_features = jnp.concatenate(
        [block_features, padded_features[:1], padded_features[3:]], axis=0
    )
    table_places = jnp.concatenate([block_places, padded_places[:1], padded_places[3:]], axis=0)
    table_rounded = table_features.astype(jnp.bfloat16)
    group = lax.axis_index("path")
    share_rows = local_rows // lax.axis_size("path")
    cotangent_share = lax.dynamic_slice_in_dim(cotangent, group * share_rows, share_rows, 0)
    all_weights = lax.all_gather(weights, "path", axis=0, tiled=True)
    all_paths = list(range(PATHS))
    slab_rows = math.gcd(share_rows, BLOCK)
    slab_numbers = jnp.arange(share_rows // slab_rows, dtype=jnp.int32)

    def slab_anchor(slab_index):
        first_row = group * share_rows + slab_index * slab_rows
        block_number = first_row // BLOCK
        within_row = first_row % BLOCK
        anchor_rows = lax.dynamic_slice_in_dim(block_places[block_number], within_row, slab_rows, 1)
        return (block_number, within_row, anchor_rows)

    def forward_slab(slab_index):
        block_number, within_row, anchor_rows = slab_anchor(slab_index)
        total = jnp.zeros((slab_rows, 9, channels), jnp.float32)
        for neighbour in range(NEIGHBOURS):
            table_slot = neighbours[block_number, neighbour]
            edge_table = edge_tensor(anchor_rows, table_places[table_slot])
            total = total + forward_terms(
                all_paths, all_weights, edge_table, table_rounded[table_slot]
            )
        return total

    message_rows = lax.map(forward_slab, slab_numbers).reshape(share_rows, 9, channels)
    gate_rows = gate_back(message_rows, cotangent_share)
    message_cotangent = lax.all_gather(gate_rows, "path", axis=0, tiled=True)
    cotangent_blocks = message_cotangent.reshape(local_blocks, BLOCK, 9, channels)
    padded_gate = with_halo(cotangent_blocks[outgoing], (("box", 0),), 1)
    table_gate = jnp.concatenate([cotangent_blocks, padded_gate[:1], padded_gate[3:]], axis=0)

    def pull_slab(slab_index):
        block_number, within_row, anchor_rows = slab_anchor(slab_index)
        own_features = lax.dynamic_slice_in_dim(
            block_features[block_number], within_row, slab_rows, 0
        )
        total = jnp.zeros((slab_rows, 9, channels), jnp.float32)
        weight_total = jnp.zeros((PATHS, BASIS, channels), jnp.float32)
        for neighbour in range(NEIGHBOURS):
            table_slot = neighbours[block_number, neighbour]
            edge_table = edge_tensor(table_places[table_slot], anchor_rows)
            contribution, weight_part = transpose_terms(
                all_paths, all_weights, edge_table, table_gate[table_slot], own_features
            )
            total = total + contribution
            weight_total = weight_total + weight_part
        return (total, weight_total)

    totals, slab_weights = lax.map(pull_slab, slab_numbers)
    grad_features = totals.reshape(share_rows, 9, channels) + cotangent_share.astype(jnp.float32)
    weight_every = lax.psum(jnp.sum(slab_weights, axis=0), ("box", "path"))
    group_paths = PATHS // lax.axis_size("path")
    weight_total = lax.dynamic_slice_in_dim(weight_every, group * group_paths, group_paths, 0)
    return (grad_features, weight_total / math.sqrt(local_rows * lax.axis_size("box")))


def solution(mesh):
    placed = (
        P("box", None, None),
        P(None, "box"),
        P("box", None, None),
        P("path", None, None),
        P("box", None),
        P("box", None),
    )
    return jax.shard_map(
        on_device,
        mesh=mesh,
        in_specs=placed,
        out_specs=(P(("box", "path"), None, None), P("path", None, None)),
        check_vma=False,
    )
```

profile of v0, /device:TPU:0, one launch (start us, length us, event | category | flops | bytes accessed | tf_op | source)
XLA Modules:
  0.0 147.7 jit_solution(1303785314537078605)
XLA Ops:
  0.6 0.8 reshape.2374
  1.4 0.7 fusion.347
  2.1 0.6 gather_fusion
  2.6 4.9 %collective-permute-start = (f32[1,3,64]{2,1,0:T(4,128)S(1)}, f32[1,3,64]{2,1,0:T(4,128)S(1)}, u32[]{:S(2)}, u32[]{:S(2)}) collective-permute-start(f32[1,3,64]{2,1,0:T(4,128)S(1)} %get-tuple-element.590), channel_id=1, source_target_pairs={{0,4},{4,8},{8,12},{12,16},{16,20},{20,24},{24,28},{1,5},{5,9},{9,... | collective-permute-start | bytes 2312 | tf_op jit(solution)/shard_map/ppermute | solution.py:51
  7.5 1.3 collective-permute-start.1
  8.8 1.7 %gather_fusion.1 = bf16[2,64,9,128]{3,1,2,0:T(8,128)(2,1)S(1)} fusion(f32[2,64,9,128]{3,1,0,2:T(8,128)} %bitcast.899, s32[1024]{0:T(1024)S(1)} %pad_clamp_fusion), kind=kCustom, calls=%fused_computation.1 | custom fusion | bytes 589832 | tf_op jit(solution)/shard_map/gather | solution.py:164
  10.5 0.7 fusion.388
  11.3 5.2 %collective-permute-start.2 = (bf16[1,64,9,128]{3,1,2,0:T(8,128)(2,1)}, bf16[1,64,9,128]{3,1,2,0:T(8,128)(2,1)}, u32[]{:S(2)}, u32[]{:S(2)}) collective-permute-start(bf16[1,64,9,128]{3,1,2,0:T(8,128)(2,1)} %get-tuple-element.509), channel_id=1, source_target_pairs={{0,4},{4,8},{8,12},{12,16},{16,20},{20,24},{24,28},{1,5},{5,9},{9,... | collective-permute-start | bytes 442376 | tf_op jit(solution)/shard_map/ppermute | solution.py:51
  16.5 1.3 collective-permute-start.3
  18.0 0.7 constant_dynamic-slice_fusion.3
  20.0 5.2 %all_gather.6 = f32[8,8,128]{2,1,0:T(8,128)S(1)} all-gather(f32[2,8,128]{2,1,0:T(8,128)S(1)} %copy-done.55), channel_id=1, replica_groups=mesh['box'=8,'path'=4] {'path'}, dimensions={0}, use_global_device_ids=true | all-gather | bytes 40960 | tf_op jit(solution)/shard_map/all_gather | solution.py:175
  25.2 0.6 slice_bitcast_fusion.210
  25.8 0.7 slice_bitcast_fusion.96
  26.4 1.6 %dynamic-slice_convert_fusion = f32[32,9,128]{2,0,1:T(8,128)} fusion(bf16[128,9,128]{2,0,1:T(8,128)(2,1)} %param.8, s32[]{:T(128)S(6)} %select_n.212), kind=kLoop, calls=%fused_computation.489 | loop fusion | flops 36864 | bytes 221188 | tf_op jit(solution)/shard_map/convert_element_type | solution.py:146
  33.4 0.8 fusion.384
  34.3 0.7 fusion.385
  35.3 0.8 fusion.386
  36.1 0.7 bitcast_negate_fusion.7
  36.8 0.6 bitcast_negate_fusion.2
  37.4 0.6 bitcast_negate_fusion
  38.1 0.6 bitcast_negate_fusion.1
  38.7 0.7 bitcast_negate_fusion.3
  39.4 0.7 bitcast_negate_fusion.4
  40.0 0.6 bitcast_negate_fusion.8
  40.6 0.6 bitcast_negate_fusion.6
  42.0 0.5 copy-done.32
  42.8 0.8 copy-done.33
  43.7 1.8 %concatenate.157 = bf16[256,320]{1,0:T(8,128)(2,1)} concatenate(bf16[256,64]{1,0:T(8,128)(2,1)} %bitcast.946, bf16[256,64]{1,0:T(8,128)(2,1)} %bitcast.945, bf16[256,64]{1,0:T(8,128)(2,1)} %bitcast.944, bf16[256,64]{1,0:T(8,128)(2,1)} %bitcast.943, bf16[256,64]{1,0:T(8,128)(2,1)} %bitcast.942), dimensions={1} | concatenate | bytes 327680 | tf_op jit(solution)/shard_map/while/body/eval_jaxpr/concatenate | solution.py:109
  45.4 1.8 %concatenate.167 = bf16[256,320]{1,0:T(8,128)(2,1)} concatenate(bf16[256,64]{1,0:T(8,128)(2,1)} %bitcast.941, bf16[256,64]{1,0:T(8,128)(2,1)} %bitcast.940, bf16[256,64]{1,0:T(8,128)(2,1)} %bitcast.939, bf16[256,64]{1,0:T(8,128)(2,1)} %bitcast.938, bf16[256,64]{1,0:T(8,128)(2,1)} %bitcast.937), dimensions={1} | concatenate | bytes 327680 | tf_op jit(solution)/shard_map/while/body/eval_jaxpr/concatenate | solution.py:109
  47.2 1.8 %concatenate.147 = bf16[256,320]{1,0:T(8,128)(2,1)} concatenate(bf16[256,64]{1,0:T(8,128)(2,1)} %bitcast.936, bf16[256,64]{1,0:T(8,128)(2,1)} %bitcast.935, bf16[256,64]{1,0:T(8,128)(2,1)} %bitcast.934, bf16[256,64]{1,0:T(8,128)(2,1)} %bitcast.933, bf16[256,64]{1,0:T(8,128)(2,1)} %bitcast.932), dimensions={1} | concatenate | bytes 327680 | tf_op jit(solution)/shard_map/while/body/eval_jaxpr/concatenate | solution.py:109
  49.0 0.8 bitcast_negate_fusion.5
  49.8 1.1 pad_maximum_fusion
  51.1 0.9 copy-done.2
  64.9 0.7 copy-done.3
  65.7 6.0 %all_gather.7 = bf16[128,9,128]{2,0,1:T(8,128)(2,1)S(1)} all-gather(bf16[32,9,128]{2,0,1:T(8,128)(2,1)S(1)} %pad_maximum_fusion.1), channel_id=1, replica_groups=mesh['box'=8,'path'=4] {'path'}, dimensions={0}, use_global_device_ids=true | all-gather | bytes 368640 | tf_op jit(solution)/shard_map/all_gather | solution.py:200
  71.8 0.7 gather_fusion.2
  72.5 4.6 %collective-permute-start.4 = (bf16[1,64,9,128]{3,1,2,0:T(8,128)(2,1)S(1)}, bf16[1,64,9,128]{3,1,2,0:T(8,128)(2,1)S(1)}, u32[]{:S(2)}, u32[]{:S(2)}) collective-permute-start(bf16[1,64,9,128]{3,1,2,0:T(8,128)(2,1)S(1)} %get-tuple-element.508), channel_id=1, source_target_pairs={{0,4},{4,8},{8,12},{12,16},{16,20},{20,24},{24,28},{1,5},{5,9},{9,... | collective-permute-start | bytes 442376 | tf_op jit(solution)/shard_map/ppermute | solution.py:51
  77.1 1.5 collective-permute-start.5
  78.6 2.1 %collective-permute-done.4 = bf16[1,64,9,128]{3,1,2,0:T(8,128)(2,1)S(1)} collective-permute-done((bf16[1,64,9,128]{3,1,2,0:T(8,128)(2,1)S(1)}, bf16[1,64,9,128]{3,1,2,0:T(8,128)(2,1)S(1)}, u32[]{:S(2)}, u32[]{:S(2)}) %collective-permute-start.4) | collective-permute-done | bytes 147488 | tf_op jit(solution)/shard_map/ppermute | solution.py:51
  80.7 5.1 %collective-permute-done.5 = bf16[1,64,9,128]{3,1,2,0:T(8,128)(2,1)S(1)} collective-permute-done((bf16[1,64,9,128]{3,1,2,0:T(8,128)(2,1)S(1)}, bf16[1,64,9,128]{3,1,2,0:T(8,128)(2,1)S(1)}, u32[]{:S(2)}, u32[]{:S(2)}) %collective-permute-start.5) | collective-permute-done | bytes 147488 | tf_op jit(solution)/shard_map/ppermute | solution.py:53
  98.1 0.4 multiply_reduce_fusion.24
  98.8 0.4 multiply_reduce_fusion.8
  99.5 0.4 multiply_reduce_fusion.5
  100.2 0.4 multiply_reduce_fusion.6
  100.9 0.5 multiply_reduce_fusion.16
  103.4 41.7 %psum.7 = f32[8,8,128]{2,1,0:T(8,128)S(1)} all-reduce(f32[8,8,128]{2,1,0:T(8,128)S(1)} %add_add_fusion.2), channel_id=1, replica_groups=mesh['box'=8,'path'=4] {'box','path'}, use_global_device_ids=true, to_apply=%region_259.260 | all-reduce | flops 8192 | bytes 65536 | tf_op jit(solution)/shard_map/psum | solution.py:224
  145.1 0.6 dynamic-slice_multiply_fusion
  146.1 1.6 %add_add_fusion = f32[32,9,128]{2,0,1:T(8,128)} fusion(f32[32,9,128]{2,0,1:T(8,128)S(1)} %constant_dynamic-update-slice_fusion.104, f32[32,9,128]{2,0,1:T(8,128)S(1)} %constant_dynamic-update-slice_fusion.72, f32[32,9,128]{2,0,1:T(8,128)S(1)} %constant_dynamic-update-slice_fusion.88, bf16[128,9,128]{2,0,1:T(8,128)(2,1)} %param.8, s32[]{:T(128)S(6)} %select_n.212), kind=kLoop, calls=%fused_computation.252 | loop fusion | flops 147456 | bytes 663556 | tf_op jit(solution)/shard_map/add | solution.py:223
  (441 shorter events, 29.4 us)
Async XLA Ops:
  2.1 9.2 %copy-start.56 = (s32[1024]{0:T(1024)}, s32[1024]{0:T(1024)S(1)}, u32[]{:S(2)}) copy-start(s32[1024]{0:T(1024)S(1)} %pad_clamp_fusion) | copy-start | bytes 12292
  2.6 29.8 %collective-permute-start = (f32[1,3,64]{2,1,0:T(4,128)S(1)}, f32[1,3,64]{2,1,0:T(4,128)S(1)}, u32[]{:S(2)}, u32[]{:S(2)}) collective-permute-start(f32[1,3,64]{2,1,0:T(4,128)S(1)} %get-tuple-element.590), channel_id=1, source_target_pairs={{0,4},{4,8},{8,12},{12,16},{16,20},{20,24},{24,28},{1,5},{5,9},{9,... | collective-permute-start | bytes 2312 | tf_op jit(solution)/shard_map/ppermute | solution.py:51
  7.5 24.9 %collective-permute-start.1 = (f32[1,3,64]{2,1,0:T(4,128)S(1)}, f32[1,3,64]{2,1,0:T(4,128)S(1)}, u32[]{:S(2)}, u32[]{:S(2)}) collective-permute-start(f32[1,3,64]{2,1,0:T(4,128)S(1)} %get-tuple-element.591), channel_id=1, source_target_pairs={{4,0},{8,4},{12,8},{16,12},{20,16},{24,20},{28,24},{5,1},{9,5},{13... | collective-permute-start | bytes 2312 | tf_op jit(solution)/shard_map/ppermute | solution.py:53
  10.5 7.5 %copy-start = (f32[128,9,128]{2,0,1:T(8,128)S(1)}, f32[128,9,128]{2,0,1:T(8,128)}, u32[]{:S(2)}) copy-start(f32[128,9,128]{2,0,1:T(8,128)} %param.6) | copy-start | bytes 1769476
  10.5 7.5 %copy-start.57 = (s32[2,3]{1,0:T(2,128)S(1)}, s32[2,3]{1,0:T(2,128)}, u32[]{:S(2)}) copy-start(s32[2,3]{1,0:T(2,128)} %param.10) | copy-start | bytes 76
  10.5 9.5 %copy-start.55 = (f32[2,8,128]{2,1,0:T(8,128)S(1)}, f32[2,8,128]{2,1,0:T(8,128)}, u32[]{:S(2)}) copy-start(f32[2,8,128]{2,1,0:T(8,128)} %param.9) | copy-start | bytes 24580
  11.3 38.5 %collective-permute-start.2 = (bf16[1,64,9,128]{3,1,2,0:T(8,128)(2,1)}, bf16[1,64,9,128]{3,1,2,0:T(8,128)(2,1)}, u32[]{:S(2)}, u32[]{:S(2)}) collective-permute-start(bf16[1,64,9,128]{3,1,2,0:T(8,128)(2,1)} %get-tuple-element.509), channel_id=1, source_target_pairs={{0,4},{4,8},{8,12},{12,16},{16,20},{20,24},{24,28},{1,5},{5,9},{9,... | collective-permute-start | bytes 442376 | tf_op jit(solution)/shard_map/ppermute | solution.py:51
  16.5 33.4 %collective-permute-start.3 = (bf16[1,64,9,128]{3,1,2,0:T(8,128)(2,1)}, bf16[1,64,9,128]{3,1,2,0:T(8,128)(2,1)}, u32[]{:S(2)}, u32[]{:S(2)}) collective-permute-start(bf16[1,64,9,128]{3,1,2,0:T(8,128)(2,1)} %get-tuple-element.510), channel_id=1, source_target_pairs={{4,0},{8,4},{12,8},{16,12},{20,16},{24,20},{28,24},{5,1},{9,5},{13... | collective-permute-start | bytes 442376 | tf_op jit(solution)/shard_map/ppermute | solution.py:53
  34.1 2.0 %copy-start.9 = (bf16[1,8,32,64]{3,2,1,0:T(8,128)(2,1)}, bf16[1,8,32,64]{3,2,1,0:T(8,128)(2,1)S(1)}, u32[]{:S(2)}) copy-start(bf16[1,8,32,64]{3,2,1,0:T(8,128)(2,1)S(1)} %get-tuple-element.487) | copy-start | bytes 98308
  34.1 5.9 %copy-start.7 = (bf16[1,8,32,64]{3,2,1,0:T(8,128)(2,1)}, bf16[1,8,32,64]{3,2,1,0:T(8,128)(2,1)S(1)}, u32[]{:S(2)}) copy-start(bf16[1,8,32,64]{3,2,1,0:T(8,128)(2,1)S(1)} %get-tuple-element.480) | copy-start | bytes 98308
  34.1 6.5 %copy-start.11 = (bf16[1,8,32,64]{3,2,1,0:T(8,128)(2,1)}, bf16[1,8,32,64]{3,2,1,0:T(8,128)(2,1)S(1)}, u32[]{:S(2)}) copy-start(bf16[1,8,32,64]{3,2,1,0:T(8,128)(2,1)S(1)} %get-tuple-element.486) | copy-start | bytes 98308
  35.1 1.7 %copy-start.17 = (bf16[1,8,32,64]{3,2,1,0:T(8,128)(2,1)}, bf16[1,8,32,64]{3,2,1,0:T(8,128)(2,1)S(1)}, u32[]{:S(2)}) copy-start(bf16[1,8,32,64]{3,2,1,0:T(8,128)(2,1)S(1)} %get-tuple-element.488) | copy-start | bytes 98308
  35.1 2.3 %copy-start.15 = (bf16[1,8,32,64]{3,2,1,0:T(8,128)(2,1)}, bf16[1,8,32,64]{3,2,1,0:T(8,128)(2,1)S(1)}, u32[]{:S(2)}) copy-start(bf16[1,8,32,64]{3,2,1,0:T(8,128)(2,1)S(1)} %get-tuple-element.494) | copy-start | bytes 98308
  35.1 3.0 %copy-start.19 = (bf16[1,8,32,64]{3,2,1,0:T(8,128)(2,1)}, bf16[1,8,32,64]{3,2,1,0:T(8,128)(2,1)S(1)}, u32[]{:S(2)}) copy-start(bf16[1,8,32,64]{3,2,1,0:T(8,128)(2,1)S(1)} %get-tuple-element.495) | copy-start | bytes 98308
  35.3 1.5 %copy-start.1 = (bf16[9,8,32,64]{3,2,1,0:T(8,128)(2,1)}, bf16[9,8,32,64]{3,2,1,0:T(8,128)(2,1)S(1)}, u32[]{:S(2)}) copy-start(bf16[9,8,32,64]{3,2,1,0:T(8,128)(2,1)S(1)} %multiply_convert_fusion.3) | copy-start | bytes 884740
  36.1 5.4 %copy-start.13 = (bf16[1,8,32,64]{3,2,1,0:T(8,128)(2,1)}, bf16[1,8,32,64]{3,2,1,0:T(8,128)(2,1)S(1)}, u32[]{:S(2)}) copy-start(bf16[1,8,32,64]{3,2,1,0:T(8,128)(2,1)S(1)} %get-tuple-element.503) | copy-start | bytes 98308
  36.1 5.4 %copy-start.21 = (bf16[1,8,32,64]{3,2,1,0:T(8,128)(2,1)}, bf16[1,8,32,64]{3,2,1,0:T(8,128)(2,1)S(1)}, u32[]{:S(2)}) copy-start(bf16[1,8,32,64]{3,2,1,0:T(8,128)(2,1)S(1)} %get-tuple-element.502) | copy-start | bytes 98308
  42.6 0.9 copy-start.33
  50.9 1.1 copy-start.2
  50.9 1.1 copy-start.51
  50.9 1.3 copy-start.39
  51.0 1.9 %copy-start.49 = (f32[8,128]{1,0:T(8,128)S(1)}, f32[8,128]{1,0:T(8,128)}, u32[]{:S(2)}) copy-start(f32[8,128]{1,0:T(8,128)} %get-tuple-element.532) | copy-start | bytes 12292
  52.0 1.2 copy-start.37
  53.2 1.2 copy-start.53
  59.0 1.0 copy-start.20
  59.0 1.0 copy-start.31
  59.3 0.9 copy-start.16
  59.3 0.9 copy-start.18
  59.8 0.9 copy-start.30
  59.9 1.0 copy-start.29
  60.2 0.9 copy-start.23
  60.2 0.9 copy-start.28
  60.2 1.1 copy-start.14
  60.2 1.1 copy-start.22
  60.9 0.9 copy-start.27
  61.1 0.9 copy-start.12
  61.1 0.9 copy-start.25
  61.3 0.9 copy-start.10
  61.9 0.9 copy-start.24
  62.2 1.0 copy-start.4
  62.6 1.0 copy-start.5
  63.0 1.0 copy-start.6
  63.3 0.9 copy-start.36
  64.7 0.9 copy-start.3
  72.5 8.2 %collective-permute-start.4 = (bf16[1,64,9,128]{3,1,2,0:T(8,128)(2,1)S(1)}, bf16[1,64,9,128]{3,1,2,0:T(8,128)(2,1)S(1)}, u32[]{:S(2)}, u32[]{:S(2)}) collective-permute-start(bf16[1,64,9,128]{3,1,2,0:T(8,128)(2,1)S(1)} %get-tuple-element.508), channel_id=1, source_target_pairs={{0,4},{4,8},{8,12},{12,16},{16,20},{20,24},{24,28},{1,5},{5,9},{9,... | collective-permute-start | bytes 442376 | tf_op jit(solution)/shard_map/ppermute | solution.py:51
  77.1 8.7 %collective-permute-start.5 = (bf16[1,64,9,128]{3,1,2,0:T(8,128)(2,1)S(1)}, bf16[1,64,9,128]{3,1,2,0:T(8,128)(2,1)S(1)}, u32[]{:S(2)}, u32[]{:S(2)}) collective-permute-start(bf16[1,64,9,128]{3,1,2,0:T(8,128)(2,1)S(1)} %get-tuple-element.507), channel_id=1, source_target_pairs={{4,0},{8,4},{12,8},{16,12},{20,16},{24,20},{28,24},{5,1},{9,5},{13... | collective-permute-start | bytes 442376 | tf_op jit(solution)/shard_map/ppermute | solution.py:53
  97.1 0.9 copy-start.52
  97.2 0.9 copy-start.54
  (16 other events, 11.7 us)
where the time goes:
time: 149 us; the launch traced here: 148 us
  blocking collectives  53 us (36%)
  matrix products  25 us (17%)
  local copies, waits for them, and re-layouts  20.3 us (14%)
  starting transfers between devices  18.7 us (13%)
  other arithmetic  14.5 us (10%)
  between operations  9.16 us (6%)
  waiting for transfers between devices  7.16 us (5%)
    psum x1, blocking collectives, on_device(): weight_every = lax.psum(jnp.sum(slab_weights, axis=0), ('box', 'path'))  41.7 us
    ppermute x3, starting transfers between devices, with_halo(): lax.ppermute(tail, axis, [(i, (i + 1) % count) for i in range(ends)])  14.6 us
    dot_general x93, matrix products, transpose_terms(): lax.dot_general(edge_table[harmonic], cotangent_rows[:, output, :], (((1,...  14.4 us
    dot_general x66, matrix products, forward_terms(): jnp.dot(jnp.concatenate(pieces, axis=1), jnp.concatenate(stacked, axis=0)...  10.6 us
    all_gather x1, blocking collectives, on_device(): message_cotangent = lax.all_gather(gate_rows, 'path', axis=0, tiled=True)  6.04 us
    unnamed x139, local copies, waits for them, and re-layouts  6.02 us
    neg x9, other arithmetic, forward_terms(): signed = edge_table[harmonic] if factor > 0 else -edge_table[harmonic]  6.01 us
    concatenate x3, local copies, waits for them, and re-layouts, forward_terms(): jnp.concatenate(pieces, axis=1)  5.3 us
  transfers between devices with their start and end apart: 6, of which 2 were waited for; matrix products, arithmetic and copies ran while one was open for 15% of the time, Pallas kernels for 0%

commit v1 on v0

--- a/solution.py
+++ b/solution.py
@@ -221,7 +221,7 @@
 
     totals, slab_weights = lax.map(pull_slab, slab_numbers)
     grad_features = totals.reshape(share_rows, 9, channels) + cotangent_share.astype(jnp.float32)
-    weight_every = lax.psum(jnp.sum(slab_weights, axis=0), ("box", "path"))
+    weight_every = jnp.sum(lax.all_gather(jnp.sum(slab_weights, axis=0), ("box", "path")), axis=0)
     group_paths = PATHS // lax.axis_size("path")
     weight_total = lax.dynamic_slice_in_dim(weight_every, group * group_paths, group_paths, 0)
     return (grad_features, weight_total / math.sqrt(local_rows * lax.axis_size("box")))

time: 149 us -> 173 us (1.16)
  waiting for transfers between devices: 7.16 us -> 60.4 us
  blocking collectives: 53 us -> 11.2 us
  between operations: 9.16 us -> 22.7 us
  local copies, waits for them, and re-layouts: 20.3 us -> 17.6 us
  other arithmetic: 14.5 us -> 16.4 us
    all_gather x0 -> x1, waiting for transfers between devices: none -> 53.3 us  [on_device(): lax.all_gather(jnp.sum(slab_weights, axis=0), ('box', 'path'))]
    psum x1 -> x0, blocking collectives: 41.7 us -> none  [on_device(): weight_every = lax.psum(jnp.sum(slab_weights, axis=0), ('box', 'path'))]
    unnamed x139, local copies, waits for them, and re-layouts: 6.02 us -> 3.2 us
  transfers between devices with their start and end apart: 6 -> 7, of which waited for: 2 -> 3; matrix products, arithmetic and copies ran while one was open for 15% -> 14% of each run, Pallas kernels for 0% -> 0%
where the time goes in v1:
time: 173 us; the launch traced here: 172 us
  waiting for transfers between devices  60.4 us (35%)
  matrix products  25.1 us (15%)
  between operations  22.7 us (13%)
  starting transfers between devices  18.7 us (11%)
  local copies, waits for them, and re-layouts  17.6 us (10%)
  other arithmetic  16.4 us (9%)
  blocking collectives  11.2 us (6%)
    all_gather x1, waiting for transfers between devices, on_device(): lax.all_gather(jnp.sum(slab_weights, axis=0), ('box', 'path'))  53.3 us
    ppermute x3, starting transfers between devices, with_halo(): lax.ppermute(tail, axis, [(i, (i + 1) % count) for i in range(ends)])  14.6 us
    dot_general x93, matrix products, transpose_terms(): lax.dot_general(edge_table[harmonic], cotangent_rows[:, output, :], (((1,...  14.4 us
    dot_general x66, matrix products, forward_terms(): jnp.dot(jnp.concatenate(pieces, axis=1), jnp.concatenate(stacked, axis=0)...  10.6 us
    all_gather x1, blocking collectives, on_device(): message_cotangent = lax.all_gather(gate_rows, 'path', axis=0, tiled=True)  6.04 us
    neg x9, other arithmetic, forward_terms(): signed = edge_table[harmonic] if factor > 0 else -edge_table[harmonic]  6.01 us
    concatenate x3, local copies, waits for them, and re-layouts, forward_terms(): jnp.concatenate(pieces, axis=1)  5.3 us
    all_gather x1, blocking collectives, on_device(): all_weights = lax.all_gather(weights, 'path', axis=0, tiled=True)  5.19 us
  transfers between devices with their start and end apart: 7, of which 3 were waited for; matrix products, arithmetic and copies ran while one was open for 14% of the time, Pallas kernels for 0%

profile of v1, /device:TPU:0, one launch (start us, length us, event | category | flops | bytes accessed | tf_op | source)
XLA Modules:
  0.0 172.1 jit_solution(9038075755418767571)
XLA Ops:
  7.2 0.8 reshape.3077
  8.0 0.7 fusion.347
  8.7 0.6 gather_fusion
  9.3 4.9 %collective-permute-start = (f32[1,3,64]{2,1,0:T(4,128)S(1)}, f32[1,3,64]{2,1,0:T(4,128)S(1)}, u32[]{:S(2)}, u32[]{:S(2)}) collective-permute-start(f32[1,3,64]{2,1,0:T(4,128)S(1)} %get-tuple-element.590), channel_id=1, source_target_pairs={{0,4},{4,8},{8,12},{12,16},{16,20},{20,24},{24,28},{1,5},{5,9},{9,... | collective-permute-start | bytes 2312 | tf_op jit(solution)/shard_map/ppermute | solution.py:51
  14.2 1.3 collective-permute-start.1
  15.5 1.7 gather_fusion.1
  17.2 0.7 fusion.388
  17.9 5.2 %collective-permute-start.2 = (bf16[1,64,9,128]{3,1,2,0:T(8,128)(2,1)}, bf16[1,64,9,128]{3,1,2,0:T(8,128)(2,1)}, u32[]{:S(2)}, u32[]{:S(2)}) collective-permute-start(bf16[1,64,9,128]{3,1,2,0:T(8,128)(2,1)} %get-tuple-element.509), channel_id=1, source_target_pairs={{0,4},{4,8},{8,12},{12,16},{16,20},{20,24},{24,28},{1,5},{5,9},{9,... | collective-permute-start | bytes 442376 | tf_op jit(solution)/shard_map/ppermute | solution.py:51
  23.1 1.3 collective-permute-start.3
  24.6 0.7 constant_dynamic-slice_fusion.3
  26.6 5.2 %all_gather.10 = f32[8,8,128]{2,1,0:T(8,128)S(1)} all-gather(f32[2,8,128]{2,1,0:T(8,128)S(1)} %copy-done.55), channel_id=1, replica_groups=mesh['box'=8,'path'=4] {'path'}, dimensions={0}, use_global_device_ids=true | all-gather | bytes 40960 | tf_op jit(solution)/shard_map/all_gather | solution.py:175
  31.8 0.6 slice_bitcast_fusion.210
  32.4 0.7 slice_bitcast_fusion.96
  33.1 1.6 dynamic-slice_convert_fusion
  40.0 0.8 fusion.384
  41.0 0.7 fusion.385
  41.9 0.8 fusion.386
  42.7 0.7 bitcast_negate_fusion.7
  43.4 0.6 bitcast_negate_fusion.2
  44.1 0.6 bitcast_negate_fusion
  44.7 0.6 bitcast_negate_fusion.1
  45.3 0.7 bitcast_negate_fusion.3
  46.0 0.7 bitcast_negate_fusion.4
  46.7 0.6 bitcast_negate_fusion.8
  47.3 0.6 bitcast_negate_fusion.6
  48.7 0.5 copy-done.32
  49.4 0.7 copy-done.33
  50.2 1.8 %concatenate.175 = bf16[256,320]{1,0:T(8,128)(2,1)} concatenate(bf16[256,64]{1,0:T(8,128)(2,1)} %bitcast.946, bf16[256,64]{1,0:T(8,128)(2,1)} %bitcast.945, bf16[256,64]{1,0:T(8,128)(2,1)} %bitcast.944, bf16[256,64]{1,0:T(8,128)(2,1)} %bitcast.943, bf16[256,64]{1,0:T(8,128)(2,1)} %bitcast.942), dimensions={1} | concatenate | bytes 327680 | tf_op jit(solution)/shard_map/while/body/eval_jaxpr/concatenate | solution.py:109
  52.0 1.8 %concatenate.185 = bf16[256,320]{1,0:T(8,128)(2,1)} concatenate(bf16[256,64]{1,0:T(8,128)(2,1)} %bitcast.941, bf16[256,64]{1,0:T(8,128)(2,1)} %bitcast.940, bf16[256,64]{1,0:T(8,128)(2,1)} %bitcast.939, bf16[256,64]{1,0:T(8,128)(2,1)} %bitcast.938, bf16[256,64]{1,0:T(8,128)(2,1)} %bitcast.937), dimensions={1} | concatenate | bytes 327680 | tf_op jit(solution)/shard_map/while/body/eval_jaxpr/concatenate | solution.py:109
  53.7 1.8 %concatenate.165 = bf16[256,320]{1,0:T(8,128)(2,1)} concatenate(bf16[256,64]{1,0:T(8,128)(2,1)} %bitcast.936, bf16[256,64]{1,0:T(8,128)(2,1)} %bitcast.935, bf16[256,64]{1,0:T(8,128)(2,1)} %bitcast.934, bf16[256,64]{1,0:T(8,128)(2,1)} %bitcast.933, bf16[256,64]{1,0:T(8,128)(2,1)} %bitcast.932), dimensions={1} | concatenate | bytes 327680 | tf_op jit(solution)/shard_map/while/body/eval_jaxpr/concatenate | solution.py:109
  55.5 0.8 bitcast_negate_fusion.5
  56.4 1.1 pad_maximum_fusion
  70.1 0.5 copy-done.3
  70.7 6.0 %all_gather.11 = bf16[128,9,128]{2,0,1:T(8,128)(2,1)S(1)} all-gather(bf16[32,9,128]{2,0,1:T(8,128)(2,1)S(1)} %pad_maximum_fusion.1), channel_id=1, replica_groups=mesh['box'=8,'path'=4] {'path'}, dimensions={0}, use_global_device_ids=true | all-gather | bytes 368640 | tf_op jit(solution)/shard_map/all_gather | solution.py:200
  76.7 0.7 gather_fusion.2
  77.5 4.6 %collective-permute-start.4 = (bf16[1,64,9,128]{3,1,2,0:T(8,128)(2,1)S(1)}, bf16[1,64,9,128]{3,1,2,0:T(8,128)(2,1)S(1)}, u32[]{:S(2)}, u32[]{:S(2)}) collective-permute-start(bf16[1,64,9,128]{3,1,2,0:T(8,128)(2,1)S(1)} %get-tuple-element.508), channel_id=1, source_target_pairs={{0,4},{4,8},{8,12},{12,16},{16,20},{20,24},{24,28},{1,5},{5,9},{9,... | collective-permute-start | bytes 442376 | tf_op jit(solution)/shard_map/ppermute | solution.py:51
  82.1 1.5 collective-permute-start.5
  83.6 2.1 %collective-permute-done.4 = bf16[1,64,9,128]{3,1,2,0:T(8,128)(2,1)S(1)} collective-permute-done((bf16[1,64,9,128]{3,1,2,0:T(8,128)(2,1)S(1)}, bf16[1,64,9,128]{3,1,2,0:T(8,128)(2,1)S(1)}, u32[]{:S(2)}, u32[]{:S(2)}) %collective-permute-start.4) | collective-permute-done | bytes 147488 | tf_op jit(solution)/shard_map/ppermute | solution.py:51
  85.7 5.1 %collective-permute-done.5 = bf16[1,64,9,128]{3,1,2,0:T(8,128)(2,1)S(1)} collective-permute-done((bf16[1,64,9,128]{3,1,2,0:T(8,128)(2,1)S(1)}, bf16[1,64,9,128]{3,1,2,0:T(8,128)(2,1)S(1)}, u32[]{:S(2)}, u32[]{:S(2)}) %collective-permute-start.5) | collective-permute-done | bytes 147488 | tf_op jit(solution)/shard_map/ppermute | solution.py:53
  103.6 0.4 multiply_reduce_fusion.8
  104.1 0.4 multiply_reduce_fusion.5
  104.7 0.4 multiply_reduce_fusion.6
  105.3 0.5 multiply_reduce_fusion.16
  107.4 0.6 add_add_fusion.2
  108.5 1.6 add_add_fusion
  110.1 53.3 %all-gather.2.cloned.1.call-done = f32[32,8,8,128]{3,2,1,0:T(8,128)} async-done(((f32[1,8,8,128]{3,2,1,0:T(8,128)}), f32[32,8,8,128]{3,2,1,0:T(8,128)}) %all-gather.2.cloned.1.call-update) | async-done | bytes 1048592 | tf_op jit(solution)/shard_map/all_gather | solution.py:224
  163.4 1.3 reduce_sum.2909
  164.7 0.6 dynamic-slice_multiply_fusion
  (444 shorter events, 28.2 us)
Async XLA Ops:
  7.2 17.4 %copy-start = (f32[128,9,128]{2,0,1:T(8,128)S(1)}, f32[128,9,128]{2,0,1:T(8,128)}, u32[]{:S(2)}) copy-start(f32[128,9,128]{2,0,1:T(8,128)} %param.6) | copy-start | bytes 1769476
  7.2 156.2 %all-gather.2.cloned.1.call-start = ((), (), s32[]{:S(2)}) async-start(), calls=%async_computation | async-start | bytes 1081344 | tf_op jit(solution)/shard_map/all_gather | solution.py:224
  8.7 15.9 %copy-start.56 = (s32[1024]{0:T(1024)}, s32[1024]{0:T(1024)S(1)}, u32[]{:S(2)}) copy-start(s32[1024]{0:T(1024)S(1)} %pad_clamp_fusion) | copy-start | bytes 12292
  9.3 29.8 %collective-permute-start = (f32[1,3,64]{2,1,0:T(4,128)S(1)}, f32[1,3,64]{2,1,0:T(4,128)S(1)}, u32[]{:S(2)}, u32[]{:S(2)}) collective-permute-start(f32[1,3,64]{2,1,0:T(4,128)S(1)} %get-tuple-element.590), channel_id=1, source_target_pairs={{0,4},{4,8},{8,12},{12,16},{16,20},{20,24},{24,28},{1,5},{5,9},{9,... | collective-permute-start | bytes 2312 | tf_op jit(solution)/shard_map/ppermute | solution.py:51
  14.2 24.9 %collective-permute-start.1 = (f32[1,3,64]{2,1,0:T(4,128)S(1)}, f32[1,3,64]{2,1,0:T(4,128)S(1)}, u32[]{:S(2)}, u32[]{:S(2)}) collective-permute-start(f32[1,3,64]{2,1,0:T(4,128)S(1)} %get-tuple-element.591), channel_id=1, source_target_pairs={{4,0},{8,4},{12,8},{16,12},{20,16},{24,20},{28,24},{5,1},{9,5},{13... | collective-permute-start | bytes 2312 | tf_op jit(solution)/shard_map/ppermute | solution.py:53
  15.5 9.2 %copy-start.57 = (s32[2,3]{1,0:T(2,128)S(1)}, s32[2,3]{1,0:T(2,128)}, u32[]{:S(2)}) copy-start(s32[2,3]{1,0:T(2,128)} %param.10) | copy-start | bytes 76
  15.5 11.1 %copy-start.55 = (f32[2,8,128]{2,1,0:T(8,128)S(1)}, f32[2,8,128]{2,1,0:T(8,128)}, u32[]{:S(2)}) copy-start(f32[2,8,128]{2,1,0:T(8,128)} %param.9) | copy-start | bytes 24580
  17.9 38.5 %collective-permute-start.2 = (bf16[1,64,9,128]{3,1,2,0:T(8,128)(2,1)}, bf16[1,64,9,128]{3,1,2,0:T(8,128)(2,1)}, u32[]{:S(2)}, u32[]{:S(2)}) collective-permute-start(bf16[1,64,9,128]{3,1,2,0:T(8,128)(2,1)} %get-tuple-element.509), channel_id=1, source_target_pairs={{0,4},{4,8},{8,12},{12,16},{16,20},{20,24},{24,28},{1,5},{5,9},{9,... | collective-permute-start | bytes 442376 | tf_op jit(solution)/shard_map/ppermute | solution.py:51
  23.1 33.3 %collective-permute-start.3 = (bf16[1,64,9,128]{3,1,2,0:T(8,128)(2,1)}, bf16[1,64,9,128]{3,1,2,0:T(8,128)(2,1)}, u32[]{:S(2)}, u32[]{:S(2)}) collective-permute-start(bf16[1,64,9,128]{3,1,2,0:T(8,128)(2,1)} %get-tuple-element.510), channel_id=1, source_target_pairs={{4,0},{8,4},{12,8},{16,12},{20,16},{24,20},{28,24},{5,1},{9,5},{13... | collective-permute-start | bytes 442376 | tf_op jit(solution)/shard_map/ppermute | solution.py:53
  40.8 2.0 %copy-start.9 = (bf16[1,8,32,64]{3,2,1,0:T(8,128)(2,1)}, bf16[1,8,32,64]{3,2,1,0:T(8,128)(2,1)S(1)}, u32[]{:S(2)}) copy-start(bf16[1,8,32,64]{3,2,1,0:T(8,128)(2,1)S(1)} %get-tuple-element.487) | copy-start | bytes 98308
  40.8 5.9 %copy-start.7 = (bf16[1,8,32,64]{3,2,1,0:T(8,128)(2,1)}, bf16[1,8,32,64]{3,2,1,0:T(8,128)(2,1)S(1)}, u32[]{:S(2)}) copy-start(bf16[1,8,32,64]{3,2,1,0:T(8,128)(2,1)S(1)} %get-tuple-element.480) | copy-start | bytes 98308
  40.8 6.5 %copy-start.11 = (bf16[1,8,32,64]{3,2,1,0:T(8,128)(2,1)}, bf16[1,8,32,64]{3,2,1,0:T(8,128)(2,1)S(1)}, u32[]{:S(2)}) copy-start(bf16[1,8,32,64]{3,2,1,0:T(8,128)(2,1)S(1)} %get-tuple-element.486) | copy-start | bytes 98308
  41.7 1.7 copy-start.17
  41.7 2.3 %copy-start.15 = (bf16[1,8,32,64]{3,2,1,0:T(8,128)(2,1)}, bf16[1,8,32,64]{3,2,1,0:T(8,128)(2,1)S(1)}, u32[]{:S(2)}) copy-start(bf16[1,8,32,64]{3,2,1,0:T(8,128)(2,1)S(1)} %get-tuple-element.494) | copy-start | bytes 98308
  41.7 3.0 %copy-start.19 = (bf16[1,8,32,64]{3,2,1,0:T(8,128)(2,1)}, bf16[1,8,32,64]{3,2,1,0:T(8,128)(2,1)S(1)}, u32[]{:S(2)}) copy-start(bf16[1,8,32,64]{3,2,1,0:T(8,128)(2,1)S(1)} %get-tuple-element.495) | copy-start | bytes 98308
  41.9 6.0 %copy-start.1 = (bf16[9,8,32,64]{3,2,1,0:T(8,128)(2,1)}, bf16[9,8,32,64]{3,2,1,0:T(8,128)(2,1)S(1)}, u32[]{:S(2)}) copy-start(bf16[9,8,32,64]{3,2,1,0:T(8,128)(2,1)S(1)} %multiply_convert_fusion.3) | copy-start | bytes 884740
  42.7 5.7 %copy-start.13 = (bf16[1,8,32,64]{3,2,1,0:T(8,128)(2,1)}, bf16[1,8,32,64]{3,2,1,0:T(8,128)(2,1)S(1)}, u32[]{:S(2)}) copy-start(bf16[1,8,32,64]{3,2,1,0:T(8,128)(2,1)S(1)} %get-tuple-element.503) | copy-start | bytes 98308
  42.7 5.7 %copy-start.21 = (bf16[1,8,32,64]{3,2,1,0:T(8,128)(2,1)}, bf16[1,8,32,64]{3,2,1,0:T(8,128)(2,1)S(1)}, u32[]{:S(2)}) copy-start(bf16[1,8,32,64]{3,2,1,0:T(8,128)(2,1)S(1)} %get-tuple-element.502) | copy-start | bytes 98308
  56.3 1.3 copy-start.2
  56.4 1.3 copy-start.51
  57.5 1.3 copy-start.49
  57.5 1.6 copy-start.37
  58.4 2.0 %copy-start.53 = (f32[8,128]{1,0:T(8,128)S(1)}, f32[8,128]{1,0:T(8,128)}, u32[]{:S(2)}) copy-start(f32[8,128]{1,0:T(8,128)} %get-tuple-element.538) | copy-start | bytes 12292
  64.0 1.9 %copy-start.20 = (bf16[1,8,32,64]{3,2,1,0:T(8,128)(2,1)S(1)}, bf16[1,8,32,64]{3,2,1,0:T(8,128)(2,1)}, u32[]{:S(2)}) copy-start(bf16[1,8,32,64]{3,2,1,0:T(8,128)(2,1)} %copy-done.19) | copy-start | bytes 98308
  64.0 1.9 %copy-start.31 = (bf16[256,64]{1,0:T(8,128)(2,1)S(1)}, bf16[256,64]{1,0:T(8,128)(2,1)}, u32[]{:S(2)}) copy-start(bf16[256,64]{1,0:T(8,128)(2,1)} %bitcast_negate_fusion.2) | copy-start | bytes 98308
  64.3 1.8 %copy-start.16 = (bf16[1,8,32,64]{3,2,1,0:T(8,128)(2,1)S(1)}, bf16[1,8,32,64]{3,2,1,0:T(8,128)(2,1)}, u32[]{:S(2)}) copy-start(bf16[1,8,32,64]{3,2,1,0:T(8,128)(2,1)} %copy-done.15) | copy-start | bytes 98308
  64.3 1.8 %copy-start.18 = (bf16[1,8,32,64]{3,2,1,0:T(8,128)(2,1)S(1)}, bf16[1,8,32,64]{3,2,1,0:T(8,128)(2,1)}, u32[]{:S(2)}) copy-start(bf16[1,8,32,64]{3,2,1,0:T(8,128)(2,1)} %copy-done.17) | copy-start | bytes 98308
  64.8 1.6 copy-start.30
  65.1 1.6 copy-start.29
  65.4 1.5 copy-start.23
  65.4 1.5 copy-start.28
  65.7 1.4 copy-start.14
  65.7 1.4 copy-start.22
  65.9 1.5 copy-start.27
  66.1 1.5 copy-start.12
  66.1 1.5 copy-start.25
  66.4 1.4 copy-start.8
  66.4 1.4 copy-start.10
  66.6 1.5 copy-start.26
  66.9 1.5 copy-start.24
  67.4 1.4 copy-start.4
  67.6 1.4 copy-start.5
  67.9 1.3 copy-start.6
  68.1 1.3 copy-start.36
  77.5 8.2 %collective-permute-start.4 = (bf16[1,64,9,128]{3,1,2,0:T(8,128)(2,1)S(1)}, bf16[1,64,9,128]{3,1,2,0:T(8,128)(2,1)S(1)}, u32[]{:S(2)}, u32[]{:S(2)}) collective-permute-start(bf16[1,64,9,128]{3,1,2,0:T(8,128)(2,1)S(1)} %get-tuple-element.508), channel_id=1, source_target_pairs={{0,4},{4,8},{8,12},{12,16},{16,20},{20,24},{24,28},{1,5},{5,9},{9,... | collective-permute-start | bytes 442376 | tf_op jit(solution)/shard_map/ppermute | solution.py:51
  82.1 8.7 %collective-permute-start.5 = (bf16[1,64,9,128]{3,1,2,0:T(8,128)(2,1)S(1)}, bf16[1,64,9,128]{3,1,2,0:T(8,128)(2,1)S(1)}, u32[]{:S(2)}, u32[]{:S(2)}) collective-permute-start(bf16[1,64,9,128]{3,1,2,0:T(8,128)(2,1)S(1)} %get-tuple-element.507), channel_id=1, source_target_pairs={{4,0},{8,4},{12,8},{16,12},{20,16},{24,20},{28,24},{5,1},{9,5},{13... | collective-permute-start | bytes 442376 | tf_op jit(solution)/shard_map/ppermute | solution.py:53
  101.5 1.5 copy-start.52
  101.6 1.5 copy-start.54
  (17 other events, 13.3 us)
Sparse Core Ops, SparseCore 0:
  108.2 55.1 all-gather.1
